TPU v7x, 256 devices: a whole 4x4x8 slice. The times are simulated.
256 devices in a mesh: outer: 16 (over y, x), inner: 16 (over z, core).
Axes of the slice: x: 4, y: 4, z: 8, core: 2. Of those that a mesh axis runs over, the one named last changes fastest.
Arguments:
- tokens: bfloat16 [65536, 8192], P(('outer', 'inner')), may hold values from -24 to 24
- upstream: bfloat16 [65536, 8192], P(('outer', 'inner')), may hold values from -24 to 24
- weights: bfloat16 [3, 8192, 256], P(None, ('outer', 'inner')), may hold values from -0.0625 to 0.0625
Outputs:
- gradients: float32 [3, 256, 8192], P(None, 'inner', 'outer')
All inputs are finite; a program needn't handle non-finite values.
Results may differ from a plain program's by a relative error of at most 0.0049.
Values may be sent and summed in bfloat16 or wider, within the bound.
A program may use at most 128 MiB of HBM per device.

v0:
```python
import jax
import jax.numpy as jnp
from jax import lax
from jax.sharding import PartitionSpec as P


def cut_along(value, dim, size):
    before, after = (value.shape[:dim], value.shape[dim + 1 :])
    return jnp.moveaxis(value.reshape(*before, size, -1, *after), dim, 0)


def piece_ends(length, count):
    step = length // count
    if step >= 8:
        step -= step % 8
    return [step * k for k in range(1, count)]


def in_order(tiles, dim):
    tiles = jnp.moveaxis(tiles, 0, dim)
    shape = tiles.shape
    return tiles.reshape(*shape[:dim], shape[dim] * shape[dim + 1], *shape[dim + 2 :])


def exchange_in_pieces(value, axis, pieces, split_dim, concat_dim):
    tiles = cut_along(value, split_dim, lax.axis_size(axis))
    cut = max(range(1, max(2, tiles.ndim - 1)), key=lambda d: tiles.shape[d])
    done = []
    for share in jnp.split(tiles, piece_ends(tiles.shape[cut], pieces), axis=cut):
        if share.size:
            done.append(lax.all_to_all(share, axis, split_axis=0, concat_axis=0, tiled=True))
    return in_order(jnp.concatenate(done, axis=cut), concat_dim)


def combine_received(received):
    return jnp.sum(received.astype(jnp.float32), axis=0)


def on_device(tokens, upstream, weights):
    full_weights = lax.all_gather(weights, ("outer", "inner"), axis=1, tiled=True)
    gate_pre = jnp.dot(tokens, full_weights[0], preferred_element_type=jnp.float32)
    up_pre = jnp.dot(tokens, full_weights[1], preferred_element_type=jnp.float32)
    hidden_grad = jnp.dot(upstream, full_weights[2], preferred_element_type=jnp.float32)
    sigmoid = jax.nn.sigmoid(gate_pre)
    activated = gate_pre * sigmoid
    hidden = (activated * up_pre).astype(jnp.bfloat16)
    grad_gate = (hidden_grad * up_pre * sigmoid * (1.0 + gate_pre * (1.0 - sigmoid))).astype(
        jnp.bfloat16
    )
    grad_up = (hidden_grad * activated).astype(jnp.bfloat16)
    stacked = jnp.stack(
        [
            jnp.dot(grad_gate.T, tokens, preferred_element_type=jnp.float32),
            jnp.dot(grad_up.T, tokens, preferred_element_type=jnp.float32),
            jnp.dot(hidden.T, upstream, preferred_element_type=jnp.float32),
        ]
    ).astype(jnp.bfloat16)
    received = exchange_in_pieces(stacked[None], "inner", 2, 2, 0)
    partial_sum = combine_received(received)
    partial_rounded = partial_sum.astype(jnp.bfloat16)
    final_pieces = lax.all_to_all(
        partial_rounded[None], "outer", split_axis=3, concat_axis=0, tiled=True
    )
    return combine_received(final_pieces)


def solution(mesh):
    placed = (
        P(("outer", "inner"), None),
        P(("outer", "inner"), None),
        P(None, ("outer", "inner"), None),
    )
    return jax.shard_map(
        on_device, mesh=mesh, in_specs=placed, out_specs=P(None, "inner", "outer"), check_vma=False
    )
```

profile of v0, /device:TPU:1, one launch (start us, length us, event | category | flops | bytes accessed | tf_op | source)
XLA Modules:
  0.0 518.0 jit_solution(4578464147569142469)
XLA Ops:
  6.5 0.0 all-gather.2.cloned.1.call-start
  6.5 0.7 all-gather.2.cloned.1.call-update
  7.3 129.5 %all-gather.2.cloned.1.call-done = bf16[3,8192,256]{2,1,0:T(8,128)(2,1)} async-done(((bf16[3,32,256]{2,1,0:T(8,128)(2,1)}), bf16[3,8192,256]{2,1,0:T(8,128)(2,1)}) %all-gather.2.cloned.1.call-update) | async-done | bytes 12582928 | tf_op jit(solution)/shard_map/all_gather | solution.py:40
  136.8 0.0 copy-start.1
  136.8 4.8 fusion
  141.6 0.0 copy-done.1
  141.6 0.0 copy-start
  141.6 3.6 fusion.2
  145.2 0.0 copy-done
  145.2 1.3 convolution_convert_fusion.1
  146.5 3.4 fusion.1
  150.0 1.3 convolution_convert_fusion.2
  151.3 1.3 convolution_convert_fusion
  152.6 1.6 maximum_bitcast_fusion
  154.3 1.3 fusion.10
  155.6 145.4 %all_to_all.19 = bf16[16,1,3,8,8192]{4,3,2,1,0:T(8,128)(2,1)} all-to-all(bf16[16,1,3,8,8192]{4,3,2,1,0:T(8,128)(2,1)S(1)} %get-tuple-element.5), channel_id=1, replica_groups=mesh['outer'=16,'inner'=16] {'inner'}, dimensions={0} | all-to-all | bytes 12582912 | tf_op jit(solution)/shard_map/all_to_all | solution.py:31
  301.0 143.6 %all_to_all.20 = bf16[16,1,3,8,8192]{4,3,2,1,0:T(8,128)(2,1)} all-to-all(bf16[16,1,3,8,8192]{4,3,2,1,0:T(8,128)(2,1)S(1)} %get-tuple-element.6), channel_id=1, replica_groups=mesh['outer'=16,'inner'=16] {'inner'}, dimensions={0} | all-to-all | bytes 12582912 | tf_op jit(solution)/shard_map/all_to_all | solution.py:31
  444.7 6.6 %maximum_reduce_fusion = bf16[3,16,8192]{2,1,0:T(8,128)(2,1)S(1)} fusion(bf16[16,1,3,8,8192]{4,3,2,1,0:T(8,128)(2,1)} %all_to_all.20, bf16[16,1,3,8,8192]{4,3,2,1,0:T(8,128)(2,1)} %all_to_all.19), kind=kLoop, calls=%fused_computation.2 | loop fusion | flops 31064064 | bytes 13369344 | tf_op jit(solution)/shard_map/reduce_sum | solution.py:36
  451.3 8.3 %copy.10 = bf16[1,3,16,8192]{2,1,0,3:T(4,128)(2,1)} copy(bf16[1,3,16,8192]{3,2,1,0:T(8,128)(2,1)S(1)} %bitcast.36) | data formatting | bytes 1572864 | tf_op jit(solution)/shard_map/broadcast_in_dim | solution.py:62
  459.6 12.8 %reshape.54 = bf16[16,2,12288]{2,1,0:T(2,128)(2,1)S(1)} reshape(bf16[8192,1,3,16]{3,2,1,0:T(4,128)(2,1)} %bitcast.31) | data formatting | bytes 1572864
  472.4 18.9 %all_to_all.21 = bf16[16,2,12288]{2,1,0:T(2,128)(2,1)S(1)} all-to-all(bf16[16,2,12288]{2,1,0:T(2,128)(2,1)S(1)} %reshape.54), channel_id=1, replica_groups=mesh['outer'=16,'inner'=16] {'outer'}, dimensions={0} | all-to-all | bytes 1572864 | tf_op jit(solution)/shard_map/all_to_all | solution.py:61
  491.3 10.7 %reshape.55 = bf16[8192,1,3,16]{3,2,1,0:T(4,128)(2,1)} reshape(bf16[16,2,12288]{2,1,0:T(2,128)(2,1)S(1)} %all_to_all.21) | data formatting | bytes 1572864
  502.1 8.1 %convert_reduce_fusion = f32[3,16,512]{1,0,2:T(4,128)S(1)} fusion(bf16[3,16,16,512]{1,0,3,2:T(4,128)(2,1)} %bitcast.32), kind=kLoop, calls=%fused_computation | loop fusion | flops 761856 | bytes 884736 | tf_op jit(solution)/shard_map/reduce_sum | solution.py:36
  510.2 0.9 copy.11
Async XLA Ops:
  6.5 130.2 %all-gather.2.cloned.1.call-start = ((), (), s32[]{:S(2)}) async-start(), calls=%async_computation.3 | async-start | bytes 12632064 | tf_op jit(solution)/shard_map/all_gather | solution.py:40
  136.8 4.9 copy-start.1
  141.6 3.6 copy-start
Sparse Core Ops, SparseCore 0:
  11.0 125.7 all-gather.1
where the time goes:
time: 518 us
  blocking collectives  308 us (59%)
  waiting for transfers between devices  130 us (25%)
  local copies, waits for them, and re-layouts  34.1 us (7%)
  other arithmetic  16.4 us (3%)
  matrix products  15.8 us (3%)
  between operations  13.5 us (3%)
    all_to_all x2, blocking collectives, exchange_in_pieces(): lax.all_to_all(share, axis, split_axis=0, concat_axis=0, tiled=True)  289 us
    all_gather x1, waiting for transfers between devices, on_device(): lax.all_gather(weights, ('outer', 'inner'), axis=1, tiled=True)  129 us
    unnamed x6, local copies, waits for them, and re-layouts  23.6 us
    all_to_all x1, blocking collectives, on_device(): lax.all_to_all(partial_rounded[None], 'outer', split_axis=3, concat_axis=...  18.9 us
    reduce_sum x2, other arithmetic, combine_received(): return jnp.sum(received.astype(jnp.float32), axis=0)  14.8 us
  transfers between devices with their start and end apart: 1, of which 1 were waited for; matrix products, arithmetic and copies ran while one was open for 0% of the time, Pallas kernels for 0%

commit v1 on v0

--- a/solution.py
+++ b/solution.py
@@ -37,7 +37,12 @@
 
 
 def on_device(tokens, upstream, weights):
-    full_weights = lax.all_gather(weights, ("outer", "inner"), axis=1, tiled=True)
+    full_weights = jnp.concatenate(
+        lax.all_to_all(
+            jnp.stack([weights] * lax.axis_size(("outer", "inner"))), ("outer", "inner"), 0, 0
+        ),
+        axis=1,
+    )
     gate_pre = jnp.dot(tokens, full_weights[0], preferred_element_type=jnp.float32)
     up_pre = jnp.dot(tokens, full_weights[1], preferred_element_type=jnp.float32)
     hidden_grad = jnp.dot(upstream, full_weights[2], preferred_element_type=jnp.float32)

time: 518 us -> 672 us (1.30)
  blocking collectives: 308 us -> 599 us
  waiting for transfers between devices: 130 us -> 0 us
  between operations: 13.5 us -> 0.09 us
  local copies, waits for them, and re-layouts: 34.1 us -> 45.1 us
    all_to_all x0 -> x1, blocking collectives: none -> 295 us  [on_device(): lax.all_to_all(jnp.stack([weights] * lax.axis_size(('outer', 'inner'))),...]
    all_gather x1 -> x0, waiting for transfers between devices: 129 us -> none  [on_device(): lax.all_gather(weights, ('outer', 'inner'), axis=1, tiled=True)]
    another operation x0 -> x1, local copies, waits for them, and re-layouts: none -> 6.98 us  [on_device(): jnp.stack([weights] * lax.axis_size(('outer', 'inner')))]
  transfers between devices with their start and end apart: 1 -> 0, of which waited for: 1 -> 0; matrix products, arithmetic and copies ran while one was open for 0% -> 0% of each run, Pallas kernels for 0% -> 0%
where the time goes in v1:
time: 672 us; the launch traced here: 671 us
  blocking collectives  599 us (89%)
  local copies, waits for them, and re-layouts  45.1 us (7%)
  other arithmetic  16.4 us (2%)
  matrix products  9.91 us (1%)
    all_to_all x1, blocking collectives, on_device(): lax.all_to_all(jnp.stack([weights] * lax.axis_size(('outer', 'inner'))),...  295 us
    all_to_all x2, blocking collectives, exchange_in_pieces(): lax.all_to_all(share, axis, split_axis=0, concat_axis=0, tiled=True)  288 us
    unnamed x6, local copies, waits for them, and re-layouts  24.6 us
    all_to_all x1, blocking collectives, on_device(): lax.all_to_all(partial_rounded[None], 'outer', split_axis=3, concat_axis=...  16.6 us
    reduce_sum x2, other arithmetic, combine_received(): return jnp.sum(received.astype(jnp.float32), axis=0)  14.8 us

profile of v1, /device:TPU:1, one launch (start us, length us, event | category | flops | bytes accessed | tf_op | source)
XLA Modules:
  0.0 671.0 jit_solution(4083375714270589148)
XLA Ops:
  0.0 7.0 %stack.10 = bf16[256,3,32,256]{3,2,1,0:T(8,128)(2,1)} broadcast(bf16[3,32,256]{2,1,0:T(8,128)(2,1)} %param.5), dimensions={1,2,3} | broadcast | bytes 12632064 | tf_op jit(solution)/shard_map/stack | solution.py:42
  7.0 295.2 %all_to_all.24 = bf16[256,3,32,256]{3,2,1,0:T(8,128)(2,1)S(1)} all-to-all(bf16[256,3,32,256]{3,2,1,0:T(8,128)(2,1)} %stack.10), channel_id=1, replica_groups=mesh['outer'=16,'inner'=16] {'outer','inner'}, dimensions={0} | all-to-all | bytes 25165824 | tf_op jit(solution)/shard_map/all_to_all | solution.py:41
  302.2 0.0 copy-start
  302.2 3.0 fusion.8
  305.2 0.1 copy-done
  305.3 3.4 fusion.11
  308.8 0.0 copy-start.1
  308.8 1.2 fusion.10
  310.0 0.9 copy-done.1
  311.0 1.2 fusion.9
  312.2 1.3 convolution_convert_fusion
  313.5 1.4 convolution_convert_fusion.2
  314.9 1.3 convolution_convert_fusion.1
  316.2 1.6 maximum_bitcast_fusion
  317.9 1.3 fusion.7
  319.2 143.9 %all_to_all.25 = bf16[16,1,3,8,8192]{4,3,2,1,0:T(8,128)(2,1)} all-to-all(bf16[16,1,3,8,8192]{4,3,2,1,0:T(8,128)(2,1)S(1)} %get-tuple-element.5), channel_id=1, replica_groups=mesh['outer'=16,'inner'=16] {'inner'}, dimensions={0} | all-to-all | bytes 12582912 | tf_op jit(solution)/shard_map/all_to_all | solution.py:31
  463.1 143.7 %all_to_all.26 = bf16[16,1,3,8,8192]{4,3,2,1,0:T(8,128)(2,1)} all-to-all(bf16[16,1,3,8,8192]{4,3,2,1,0:T(8,128)(2,1)S(1)} %get-tuple-element.6), channel_id=1, replica_groups=mesh['outer'=16,'inner'=16] {'inner'}, dimensions={0} | all-to-all | bytes 12582912 | tf_op jit(solution)/shard_map/all_to_all | solution.py:31
  606.9 6.6 maximum_reduce_fusion
  613.5 8.2 %copy.10 = bf16[1,3,16,8192]{2,1,0,3:T(4,128)(2,1)} copy(bf16[1,3,16,8192]{3,2,1,0:T(8,128)(2,1)S(1)} %bitcast.38) | data formatting | bytes 1572864 | tf_op jit(solution)/shard_map/broadcast_in_dim | solution.py:67
  621.7 12.8 %reshape.67 = bf16[16,2,12288]{2,1,0:T(2,128)(2,1)S(1)} reshape(bf16[8192,1,3,16]{3,2,1,0:T(4,128)(2,1)} %bitcast.30) | data formatting | bytes 1572864
  634.5 16.6 %all_to_all.27 = bf16[16,2,12288]{2,1,0:T(2,128)(2,1)S(1)} all-to-all(bf16[16,2,12288]{2,1,0:T(2,128)(2,1)S(1)} %reshape.67), channel_id=1, replica_groups=mesh['outer'=16,'inner'=16] {'outer'}, dimensions={0} | all-to-all | bytes 1572864 | tf_op jit(solution)/shard_map/all_to_all | solution.py:66
  651.2 10.8 %reshape.68 = bf16[8192,1,3,16]{3,2,1,0:T(4,128)(2,1)} reshape(bf16[16,2,12288]{2,1,0:T(2,128)(2,1)S(1)} %all_to_all.27) | data formatting | bytes 1572864
  661.9 8.1 %convert_reduce_fusion = f32[3,16,512]{1,0,2:T(4,128)S(1)} fusion(bf16[3,16,16,512]{1,0,3,2:T(4,128)(2,1)} %bitcast.31), kind=kLoop, calls=%fused_computation | loop fusion | flops 761856 | bytes 884736 | tf_op jit(solution)/shard_map/reduce_sum | solution.py:36
  670.1 0.9 copy.11
Async XLA Ops:
  302.2 3.2 copy-start
  308.8 2.2 copy-start.1

commit v2 on v0

--- a/solution.py
+++ b/solution.py
@@ -2,6 +2,18 @@
 import jax.numpy as jnp
 from jax import lax
 from jax.sharding import PartitionSpec as P
+
+
+def split_up(x, dim, devices):
+    dims = x.shape
+    pieces = x.reshape(*dims[:dim], devices, dims[dim] // devices, *dims[dim + 1 :])
+    return jnp.moveaxis(pieces, dim, 0)
+
+
+def laid_out(parts, dim):
+    parts = jnp.moveaxis(parts, 0, dim)
+    dims = parts.shape
+    return parts.reshape(*dims[:dim], dims[dim] * dims[dim + 1], *dims[dim + 2 :])
 
 
 def cut_along(value, dim, size):
@@ -58,9 +70,16 @@
     received = exchange_in_pieces(stacked[None], "inner", 2, 2, 0)
     partial_sum = combine_received(received)
     partial_rounded = partial_sum.astype(jnp.bfloat16)
-    final_pieces = lax.all_to_all(
-        partial_rounded[None], "outer", split_axis=3, concat_axis=0, tiled=True
-    )
+    size_2, index = (lax.axis_size("outer"), lax.axis_index("outer"))
+    tiles_2 = split_up(partial_rounded[None], 3, size_2)
+    finished = [tiles_2[index]]
+    for lap in range(1, size_2):
+        sent = tiles_2[(index + lap) % size_2]
+        finished.append(
+            lax.ppermute(sent, "outer", [(i, (i + lap) % size_2) for i in range(size_2)])
+        )
+    tiles_2 = jnp.stack(finished)[(index - jnp.arange(size_2)) % size_2]
+    final_pieces = laid_out(tiles_2, 0)
     return combine_received(final_pieces)
 
 

time: 518 us -> 496 us (0.958)
  blocking collectives: 308 us -> 145 us
  waiting for transfers between devices: 130 us -> 268 us
  starting transfers between devices: 0.01 us -> 31.7 us
  local copies, waits for them, and re-layouts: 34.1 us -> 7.06 us
  other arithmetic: 16.4 us -> 9.02 us
    all_to_all x2 -> x1, blocking collectives: 289 us -> 145 us  [exchange_in_pieces(): lax.all_to_all(share, axis, split_axis=0, concat_axis=0, tiled=True)]
    all_to_all x0 -> x1, waiting for transfers between devices: none -> 137 us  [exchange_in_pieces(): lax.all_to_all(share, axis, split_axis=0, concat_axis=0, tiled=True)]
    ppermute x0 -> x15, starting transfers between devices: none -> 27 us  [on_device(): lax.ppermute(sent, 'outer', [(i, (i + lap) % size_2) for i in range(size_...]
    unnamed x6 -> x35, local copies, waits for them, and re-layouts: 23.6 us -> 0.49 us
    all_to_all x1 -> x0, blocking collectives: 18.9 us -> none  [on_device(): lax.all_to_all(partial_rounded[None], 'outer', split_axis=3, concat_axis=...]
    broadcast_in_dim x1 -> x0, local copies, waits for them, and re-layouts: 8.27 us -> none  [on_device(): partial_rounded[None]]
    reduce_sum x2, other arithmetic: 14.8 us -> 7.39 us  [combine_received(): return jnp.sum(received.astype(jnp.float32), axis=0)]
  transfers between devices with their start and end apart: 1 -> 17, of which waited for: 1 -> 4; matrix products, arithmetic and copies ran while one was open for 0% -> 0% of each run, Pallas kernels for 0% -> 0%
where the time goes in v2:
time: 496 us; the launch traced here: 491 us
  waiting for transfers between devices  268 us (54%)
  blocking collectives  145 us (29%)
  starting transfers between devices  31.7 us (6%)
  matrix products  15.8 us (3%)
  between operations  13.9 us (3%)
  other arithmetic  9.02 us (2%)
  local copies, waits for them, and re-layouts  7.06 us (1%)
    all_to_all x1, blocking collectives, exchange_in_pieces(): lax.all_to_all(share, axis, split_axis=0, concat_axis=0, tiled=True)  145 us
    all_to_all x1, waiting for transfers between devices, exchange_in_pieces(): lax.all_to_all(share, axis, split_axis=0, concat_axis=0, tiled=True)  137 us
    all_gather x1, waiting for transfers between devices, on_device(): lax.all_gather(weights, ('outer', 'inner'), axis=1, tiled=True)  129 us
    ppermute x15, starting transfers between devices, on_device(): lax.ppermute(sent, 'outer', [(i, (i + lap) % size_2) for i in range(size_...  27 us
  transfers between devices with their start and end apart: 17, of which 4 were waited for; matrix products, arithmetic and copies ran while one was open for 0% of the time, Pallas kernels for 0%

profile of v2, /device:TPU:1, one launch (start us, length us, event | category | flops | bytes accessed | tf_op | source)
XLA Modules:
  0.0 491.2 jit_solution(13697698417208293603)
XLA Ops:
  6.5 0.7 all-gather.2.cloned.1.call-update
  7.3 129.5 %all-gather.2.cloned.1.call-done = bf16[3,8192,256]{2,1,0:T(8,128)(2,1)} async-done(((bf16[3,32,256]{2,1,0:T(8,128)(2,1)}), bf16[3,8192,256]{2,1,0:T(8,128)(2,1)}) %all-gather.2.cloned.1.call-update) | async-done | bytes 12582928 | tf_op jit(solution)/shard_map/all_gather | solution.py:52
  136.8 4.8 fusion.1
  141.6 3.6 fusion
  145.2 1.3 convolution_convert_fusion
  146.5 3.4 fusion.2
  150.0 1.3 convolution_convert_fusion.1
  151.3 1.3 convolution_convert_fusion.2
  152.6 1.6 maximum_bitcast_fusion
  154.3 3.6 fusion.12
  157.9 145.4 %all_to_all.10 = bf16[16,1,3,8,8192]{4,3,2,1,0:T(8,128)(2,1)} all-to-all(bf16[16,1,3,8,8192]{4,3,2,1,0:T(8,128)(2,1)S(1)} %get-tuple-element.6), channel_id=1, replica_groups=mesh['outer'=16,'inner'=16] {'inner'}, dimensions={0} | all-to-all | bytes 12582912 | tf_op jit(solution)/shard_map/all_to_all | solution.py:43
  303.3 4.7 all-to-all-start
  308.3 136.8 %all-to-all-done = bf16[16,1,3,8,8192]{4,3,2,1,0:T(8,128)(2,1)} async-done(((bf16[16,1,3,8,8192]{4,3,2,1,0:T(8,128)(2,1)}), bf16[16,1,3,8,8192]{4,3,2,1,0:T(8,128)(2,1)}, u32[]{:S(2)}, u32[]{:S(2)}) %all-to-all-start) | async-done | bytes 6291488 | tf_op jit(solution)/shard_map/all_to_all | solution.py:43
  445.1 6.6 %maximum_reduce_fusion = bf16[3,16,8192]{2,1,0:T(8,128)(2,1)S(1)} fusion(bf16[16,1,3,8,8192]{4,3,2,1,0:T(8,128)(2,1)} %all_to_all.10, bf16[16,1,3,8,8192]{4,3,2,1,0:T(8,128)(2,1)} %all-to-all-done), kind=kLoop, calls=%fused_computation.2 | loop fusion | flops 31064064 | bytes 13369344 | tf_op jit(solution)/shard_map/reduce_sum | solution.py:48
  452.0 2.3 constant_dynamic-slice_fusion
  454.3 0.7 collective-permute-start
  455.0 2.5 collective-permute-start.1
  457.5 0.9 collective-permute-start.2
  458.5 1.2 collective-permute-start.3
  459.7 1.1 collective-permute-start.4
  461.0 2.1 collective-permute-start.5
  463.1 3.9 collective-permute-start.6
  467.0 1.7 collective-permute-start.7
  468.7 0.6 collective-permute-start.8
  469.3 3.3 collective-permute-start.9
  472.6 4.2 collective-permute-start.10
  476.9 0.6 collective-permute-start.11
  477.6 1.0 collective-permute-start.13
  478.6 3.1 collective-permute-start.14
  482.3 0.7 collective-permute-done.14
  483.0 0.6 gather_fusion
  483.6 0.8 convert_reduce_fusion
  (54 shorter events, 1.1 us)
Async XLA Ops:
  6.5 130.2 %all-gather.2.cloned.1.call-start = ((), (), s32[]{:S(2)}) async-start(), calls=%async_computation.2 | async-start | bytes 12632064 | tf_op jit(solution)/shard_map/all_gather | solution.py:52
  136.8 4.9 copy-start
  141.6 3.6 copy-start.1
  303.3 141.8 %all-to-all-start = ((bf16[16,1,3,8,8192]{4,3,2,1,0:T(8,128)(2,1)}), bf16[16,1,3,8,8192]{4,3,2,1,0:T(8,128)(2,1)}, u32[]{:S(2)}, u32[]{:S(2)}) async-start(bf16[16,1,3,8,8192]{4,3,2,1,0:T(8,128)(2,1)} %get-tuple-element.5), calls=%async_computation | async-start | bytes 12582912 | tf_op jit(solution)/shard_map/all_to_all | solution.py:43
  454.3 6.7 %collective-permute-start = (bf16[1,3,16,512]{3,2,1,0:T(8,128)(2,1)S(1)}, bf16[1,3,16,512]{3,2,1,0:T(8,128)(2,1)S(1)}, u32[]{:S(2)}, u32[]{:S(2)}) collective-permute-start(bf16[1,3,16,512]{3,2,1,0:T(8,128)(2,1)S(1)} %bitcast.130), channel_id=1, source_target_pairs={{0,16},{16,32},{32,48},{48,64},{64,80},{80,96},{96,112},{112,128},... | collective-permute-start | bytes 147464 | tf_op jit(solution)/shard_map/ppermute | solution.py:79
  455.0 8.1 %collective-permute-start.1 = (bf16[1,3,16,512]{3,2,1,0:T(8,128)(2,1)S(1)}, bf16[1,3,16,512]{3,2,1,0:T(8,128)(2,1)S(1)}, u32[]{:S(2)}, u32[]{:S(2)}) collective-permute-start(bf16[1,3,16,512]{3,2,1,0:T(8,128)(2,1)S(1)} %bitcast.129), channel_id=1, source_target_pairs={{0,32},{16,48},{32,64},{48,80},{64,96},{80,112},{96,128},{112,144}... | collective-permute-start | bytes 147464 | tf_op jit(solution)/shard_map/ppermute | solution.py:79
  457.5 9.5 %collective-permute-start.2 = (bf16[1,3,16,512]{3,2,1,0:T(8,128)(2,1)S(1)}, bf16[1,3,16,512]{3,2,1,0:T(8,128)(2,1)S(1)}, u32[]{:S(2)}, u32[]{:S(2)}) collective-permute-start(bf16[1,3,16,512]{3,2,1,0:T(8,128)(2,1)S(1)} %bitcast.128), channel_id=1, source_target_pairs={{0,48},{16,64},{32,80},{48,96},{64,112},{80,128},{96,144},{112,160... | collective-permute-start | bytes 147464 | tf_op jit(solution)/shard_map/ppermute | solution.py:79
  458.5 10.2 %collective-permute-start.3 = (bf16[1,3,16,512]{3,2,1,0:T(8,128)(2,1)S(1)}, bf16[1,3,16,512]{3,2,1,0:T(8,128)(2,1)S(1)}, u32[]{:S(2)}, u32[]{:S(2)}) collective-permute-start(bf16[1,3,16,512]{3,2,1,0:T(8,128)(2,1)S(1)} %bitcast.127), channel_id=1, source_target_pairs={{0,64},{16,80},{32,96},{48,112},{64,128},{80,144},{96,160},{112,17... | collective-permute-start | bytes 147464 | tf_op jit(solution)/shard_map/ppermute | solution.py:79
  459.7 9.6 %collective-permute-start.4 = (bf16[1,3,16,512]{3,2,1,0:T(8,128)(2,1)S(1)}, bf16[1,3,16,512]{3,2,1,0:T(8,128)(2,1)S(1)}, u32[]{:S(2)}, u32[]{:S(2)}) collective-permute-start(bf16[1,3,16,512]{3,2,1,0:T(8,128)(2,1)S(1)} %bitcast.126), channel_id=1, source_target_pairs={{0,80},{16,96},{32,112},{48,128},{64,144},{80,160},{96,176},{112,1... | collective-permute-start | bytes 147464 | tf_op jit(solution)/shard_map/ppermute | solution.py:79
  461.0 11.6 %collective-permute-start.5 = (bf16[1,3,16,512]{3,2,1,0:T(8,128)(2,1)S(1)}, bf16[1,3,16,512]{3,2,1,0:T(8,128)(2,1)S(1)}, u32[]{:S(2)}, u32[]{:S(2)}) collective-permute-start(bf16[1,3,16,512]{3,2,1,0:T(8,128)(2,1)S(1)} %bitcast.125), channel_id=1, source_target_pairs={{0,96},{16,112},{32,128},{48,144},{64,160},{80,176},{96,192},{112,... | collective-permute-start | bytes 147464 | tf_op jit(solution)/shard_map/ppermute | solution.py:79
  463.1 13.7 %collective-permute-start.6 = (bf16[1,3,16,512]{3,2,1,0:T(8,128)(2,1)S(1)}, bf16[1,3,16,512]{3,2,1,0:T(8,128)(2,1)S(1)}, u32[]{:S(2)}, u32[]{:S(2)}) collective-permute-start(bf16[1,3,16,512]{3,2,1,0:T(8,128)(2,1)S(1)} %bitcast.124), channel_id=1, source_target_pairs={{0,112},{16,128},{32,144},{48,160},{64,176},{80,192},{96,208},{112... | collective-permute-start | bytes 147464 | tf_op jit(solution)/shard_map/ppermute | solution.py:79
  467.0 10.4 %collective-permute-start.7 = (bf16[1,3,16,512]{3,2,1,0:T(8,128)(2,1)S(1)}, bf16[1,3,16,512]{3,2,1,0:T(8,128)(2,1)S(1)}, u32[]{:S(2)}, u32[]{:S(2)}) collective-permute-start(bf16[1,3,16,512]{3,2,1,0:T(8,128)(2,1)S(1)} %bitcast.123), channel_id=1, source_target_pairs={{0,128},{16,144},{32,160},{48,176},{64,192},{80,208},{96,224},{112... | collective-permute-start | bytes 147464 | tf_op jit(solution)/shard_map/ppermute | solution.py:79
  468.7 8.9 %collective-permute-start.8 = (bf16[1,3,16,512]{3,2,1,0:T(8,128)(2,1)S(1)}, bf16[1,3,16,512]{3,2,1,0:T(8,128)(2,1)S(1)}, u32[]{:S(2)}, u32[]{:S(2)}) collective-permute-start(bf16[1,3,16,512]{3,2,1,0:T(8,128)(2,1)S(1)} %bitcast.122), channel_id=1, source_target_pairs={{0,144},{16,160},{32,176},{48,192},{64,208},{80,224},{96,240},{112... | collective-permute-start | bytes 147464 | tf_op jit(solution)/shard_map/ppermute | solution.py:79
  469.3 9.3 %collective-permute-start.9 = (bf16[1,3,16,512]{3,2,1,0:T(8,128)(2,1)S(1)}, bf16[1,3,16,512]{3,2,1,0:T(8,128)(2,1)S(1)}, u32[]{:S(2)}, u32[]{:S(2)}) collective-permute-start(bf16[1,3,16,512]{3,2,1,0:T(8,128)(2,1)S(1)} %bitcast.121), channel_id=1, source_target_pairs={{0,160},{16,176},{32,192},{48,208},{64,224},{80,240},{96,0},{112,1... | collective-permute-start | bytes 147464 | tf_op jit(solution)/shard_map/ppermute | solution.py:79
  472.6 9.1 %collective-permute-start.10 = (bf16[1,3,16,512]{3,2,1,0:T(8,128)(2,1)S(1)}, bf16[1,3,16,512]{3,2,1,0:T(8,128)(2,1)S(1)}, u32[]{:S(2)}, u32[]{:S(2)}) collective-permute-start(bf16[1,3,16,512]{3,2,1,0:T(8,128)(2,1)S(1)} %bitcast.120), channel_id=1, source_target_pairs={{0,176},{16,192},{32,208},{48,224},{64,240},{80,0},{96,16},{112,32... | collective-permute-start | bytes 147464 | tf_op jit(solution)/shard_map/ppermute | solution.py:79
  476.9 4.9 collective-permute-start.11
  477.5 4.8 collective-permute-start.12
  477.6 4.6 collective-permute-start.13
  478.6 4.4 collective-permute-start.14
Sparse Core Ops, SparseCore 0:
  11.0 125.7 all-gather.1
